TPU v7x, 32 devices: a whole 2x2x4 slice. The times are simulated.
32 devices in a mesh: dp: 4 (over y, x), tp: 8 (over z, core).
Axes of the slice: x: 2, y: 2, z: 4, core: 2. Of those that a mesh axis runs over, the one named last changes fastest.
Arguments:
- hidden_in: bfloat16 [4, 32, 4096], P(None, 'dp'), may hold values from -6 to 6
- pre_gain: float32 [4096], replicated, may hold values from 0.25 to 1.75
- w_zx: bfloat16 [4096, 2, 8192], P(None, None, 'tp'), may hold values from -0.09375 to 0.09375
- zx_codes: bfloat16 [4096, 2, 8192], P(('dp', 'tp')), may hold values from -4 to 4
- zx_exponents: int32 [32, 2, 64], P('dp', None, 'tp'), may hold values from -9 to -6
- w_bc: bfloat16 [4096, 2048], P(None, 'tp'), may hold values from -0.09375 to 0.09375
- w_dt: bfloat16 [4096, 128], P(None, 'tp'), may hold values from -0.09375 to 0.09375
- conv_x: float32 [5, 8192], P(None, 'tp'), may hold values from -0.6 to 0.6
- conv_bc: float32 [5, 2048], P(None, 'tp'), may hold values from -0.6 to 0.6
- dt_bias: float32 [128], P('tp'), may hold values from -2 to 0.5
- decay_rate: float32 [128], P('tp'), may hold values from 0.05 to 2
- skip_gain: float32 [128], P('tp'), may hold values from 0.5 to 1.5
- conv_state_x: bfloat16 [32, 3, 8192], P('dp', None, 'tp'), may hold values from -6 to 6
- conv_state_bc: bfloat16 [32, 3, 2048], P('dp', None, 'tp'), may hold values from -6 to 6
- ssm_state: float32 [32, 128, 64, 256], P('dp', 'tp'), may hold values from -6 to 6
- norm_gain: float32 [8192], P('tp'), may hold values from 0.25 to 1.75
- w_out: bfloat16 [8192, 4096], P('tp'), may hold values from -0.0625 to 0.0625
- out_codes: bfloat16 [8192, 4096], P('tp', 'dp'), may hold values from -4 to 4
- out_exponents: int32 [64, 32], P('tp', 'dp'), may hold values from -7 to -4
Outputs:
- mixed: bfloat16 [4, 32, 4096], P(None, 'dp', 'tp')
- final_state: float32 [32, 128, 64, 256], P('dp', 'tp')
All inputs are finite; a program needn't handle non-finite values.
Results may differ from a plain program's by a relative error of at most 0.014.
Values may be sent and summed in bfloat16 or wider, within the bound.
A program may use at most 192 MiB of HBM per device.

v0:
```python
import jax
import jax.numpy as jnp
from jax import lax
from jax.sharding import PartitionSpec as P

D = 4096
H = 128
G = 4
BLK = 128
STEPS = 4
DI = 8192
EPS = 1e-05


def decode_pairs(codes, exponents, block):
    rows, pair, cols = codes.shape
    blocked = codes.astype(jnp.float32).reshape(rows // block, block, pair, cols // block, block)
    scales = jnp.exp2(exponents.astype(jnp.float32))
    return (blocked * scales[:, None, :, :, None]).reshape(rows, pair, cols)


def decode_matrix(codes, exponents, block):
    rows, cols = codes.shape
    blocked = codes.astype(jnp.float32).reshape(rows // block, block, cols // block, block)
    scales = jnp.exp2(exponents.astype(jnp.float32))
    return (blocked * scales[:, None, :, None]).reshape(rows, cols)


def conv_step(history, fresh, params):
    window = jnp.concatenate([history, fresh[:, None, :]], axis=1)
    mixed = jnp.sum(window * params[:4][None], axis=1) + params[4]
    return (jax.nn.silu(mixed), window[:, 1:])


def body(
    hidden_in,
    pre_gain,
    w_zx,
    zx_codes,
    zx_exponents,
    w_bc,
    w_dt,
    conv_x,
    conv_bc,
    dt_bias,
    decay_rate,
    skip_gain,
    conv_state_x,
    conv_state_bc,
    ssm_state,
    norm_gain,
    w_out,
    out_codes,
    out_exponents,
):
    slot = lax.axis_index("tp")
    tp_count = lax.axis_size("tp")
    traded = lax.all_to_all(zx_codes, "tp", split_axis=2, concat_axis=0, tiled=True)
    zx_delta = decode_pairs(traded, zx_exponents, BLK)
    local_cols = traded.shape[2]
    gathered = lax.all_gather(zx_delta.astype(jnp.bfloat16), "dp", axis=0, tiled=True)
    zx_weights = (
        (w_zx.astype(jnp.float32) + gathered.astype(jnp.float32))
        .astype(jnp.bfloat16)
        .reshape(D, 2 * local_cols)
    )
    out_piece = decode_matrix(out_codes, out_exponents, BLK).astype(jnp.bfloat16)
    out_full = lax.all_gather(out_piece, "dp", axis=1, tiled=True)
    new_out = (w_out.astype(jnp.float32) + out_full.astype(jnp.float32)).astype(jnp.bfloat16)
    heads_here = ssm_state.shape[1]
    states_n = ssm_state.shape[3]
    group = slot * heads_here // (H // G)
    group_mask = (jnp.arange(G) == group).astype(jnp.float32)
    history_x = conv_state_x.astype(jnp.float32)
    history_bc = conv_state_bc.astype(jnp.float32)
    state = ssm_state
    results = []
    carried = None
    for step in range(STEPS):
        x = hidden_in[step].astype(jnp.float32)
        if step > 0:
            x = x + carried.astype(jnp.float32)
        rows = x.shape[0]
        normed = (x * lax.rsqrt(jnp.mean(x * x, -1, keepdims=True) + EPS) * pre_gain).astype(
            jnp.bfloat16
        )
        zx = jnp.dot(normed, zx_weights, preferred_element_type=jnp.float32)
        zx = zx.reshape(rows, 2, local_cols)
        gate = zx[:, 0]
        inner = zx[:, 1]
        bc_raw = jnp.dot(normed, w_bc, preferred_element_type=jnp.float32)
        dt_raw = jnp.dot(normed, w_dt, preferred_element_type=jnp.float32)
        conv_inner, history_x = conv_step(history_x, inner, conv_x)
        conv_piece, history_bc = conv_step(history_bc, bc_raw, conv_bc)
        bc_all = lax.all_gather(conv_piece, "tp", axis=1, tiled=True)
        b_group = lax.dynamic_slice_in_dim(bc_all, group * states_n, states_n, 1)
        c_group = lax.dynamic_slice_in_dim(bc_all, G * states_n + group * states_n, states_n, 1)
        step_size = jax.nn.softplus(dt_raw + dt_bias)
        decay = jnp.exp(-step_size * decay_rate)
        inner_heads = conv_inner.reshape(rows, heads_here, -1)
        state = (
            decay[:, :, None, None] * state
            + (step_size[:, :, None] * inner_heads)[:, :, :, None] * b_group[:, None, None, :]
        )
        read = (
            jnp.einsum("rhpn,rn->rhp", state, c_group, precision=lax.Precision.HIGHEST)
            + skip_gain[:, None] * inner_heads
        )
        gated = read.reshape(rows, local_cols) * jax.nn.silu(gate)
        squares = jnp.sum(gated * gated, -1)
        totals = lax.psum(squares[:, None] * group_mask, "tp")
        mean_sq = jnp.sum(totals * group_mask, -1) / (DI // G)
        scaled = (gated * lax.rsqrt(mean_sq + EPS)[:, None] * norm_gain).astype(jnp.bfloat16)
        partial_value = jnp.dot(scaled, new_out, preferred_element_type=jnp.float32)
        whole = lax.psum(partial_value, "tp").astype(jnp.bfloat16)
        width = partial_value.shape[1] // tp_count
        results.append(lax.dynamic_slice_in_dim(whole, slot * width, width, 1))
        carried = whole
    return (jnp.stack(results), state)


def solution(mesh):
    return jax.shard_map(
        body,
        mesh=mesh,
        in_specs=(
            P(None, "dp", None),
            P(),
            P(None, None, "tp"),
            P(("dp", "tp"), None, None),
            P("dp", None, "tp"),
            P(None, "tp"),
            P(None, "tp"),
            P(None, "tp"),
            P(None, "tp"),
            P("tp"),
            P("tp"),
            P("tp"),
            P("dp", None, "tp"),
            P("dp", None, "tp"),
            P("dp", "tp", None, None),
            P("tp"),
            P("tp", None),
            P("tp", "dp"),
            P("tp", "dp"),
        ),
        out_specs=(P(None, "dp", "tp"), P("dp", "tp", None, None)),
        check_vma=False,
    )
```

profile of v0, /device:TPU:0, one launch (start us, length us, event | category | flops | bytes accessed | tf_op | source)
XLA Modules:
  0.0 712.7 jit_solution(7525767807919478908)
XLA Ops:
  7.2 0.8 multiply_exponential_fusion.4
  8.1 0.3 mul.639
  8.4 4.1 fusion.3
  12.6 15.0 %copy.29 = bf16[128,2,8192]{0,1,2:T(2,128)(2,1)} copy(bf16[128,2,8192]{2,1,0:T(2,128)(2,1)} %param.22) | data formatting | bytes 8388608 | tf_op args[3]
  27.6 6.4 all-to-all-start
  34.1 4.0 mul.609
  38.1 10.8 %mul.610 = f32[1024,2,1024]{2,1,0:T(2,128)} reshape(f32[8,128,2,8,128]{4,3,2,1,0:T(8,128)} %mul.609) | data formatting | bytes 16777216 | tf_op jit(solution)/shard_map/mul | solution.py:19
  48.8 79.2 %all-to-all-done = bf16[128,2,8192]{0,1,2:T(2,128)(2,1)} async-done(((bf16[128,2,8192]{0,1,2:T(2,128)(2,1)}), bf16[128,2,8192]{0,1,2:T(2,128)(2,1)}, u32[]{:S(2)}, u32[]{:S(2)}) %all-to-all-start) | async-done | bytes 4194336 | tf_op jit(solution)/shard_map/all_to_all | solution.py:58
  128.1 8.5 %convert_bitcast_fusion = f32[8,128,2,1024]{1,2,3,0:T(2,128)} fusion(bf16[128,2,8,1024]{0,1,3,2:T(2,128)(2,1)} %bitcast.39), kind=kLoop, calls=%fused_computation.2 | loop fusion | flops 2097152 | bytes 12582912 | tf_op jit(solution)/shard_map/convert_element_type | solution.py:17
  136.5 17.1 %copy.30 = f32[8,128,2,1024]{3,2,1,0:T(2,128)} copy(f32[8,128,2,1024]{1,2,3,0:T(2,128)} %convert_bitcast_fusion) | data formatting | bytes 16777216 | tf_op jit(solution)/shard_map/convert_element_type | solution.py:17
  153.7 9.0 %fusion = bf16[1024,2,1024]{2,1,0:T(2,128)(2,1)} fusion(f32[1024,2,1024]{2,1,0:T(2,128)} %mul.610, f32[8,128,2,1024]{3,2,1,0:T(2,128)} %copy.30), kind=kLoop, calls=%fused_computation.4 | loop fusion | flops 4194304 | bytes 20971520 | tf_op jit(solution)/shard_map/convert_element_type | solution.py:61
  163.0 0.1 fusion.13
  163.2 0.4 convolution_bitcast_fusion.3
  163.6 14.2 %all_gather.19 = f32[8,2048]{1,0:T(8,128)S(1)} all-gather(f32[8,256]{1,0:T(8,128)S(1)} %divide_multiply_fusion.7), channel_id=1, replica_groups=mesh['dp'=4,'tp'=8] {'tp'}, dimensions={1}, use_global_device_ids=true | all-gather | bytes 73728 | tf_op jit(solution)/shard_map/all_gather | solution.py:95
  177.8 0.2 multiply_exponential_fusion.5
  178.1 10.1 %add_convert_fusion.1 = bf16[1024,4096]{1,0:T(8,128)(2,1)} fusion(bf16[1024,4096]{1,0:T(8,128)(2,1)} %all-gather.5.cloned.1.call-done, bf16[1024,4096]{1,0:T(8,128)(2,1)} %param.35), kind=kLoop, calls=%fused_computation.1 | loop fusion | flops 16777216 | bytes 25165824 | tf_op jit(solution)/shard_map/convert_element_type | solution.py:69
  188.2 131.0 %all-gather.3.cloned.1.call-done = bf16[4096,2,1024]{2,1,0:T(2,128)(2,1)} async-done(((bf16[1024,2,1024]{2,1,0:T(2,128)(2,1)}), bf16[4096,2,1024]{2,1,0:T(2,128)(2,1)}) %all-gather.3.cloned.1.call-update) | async-done | bytes 16777232 | tf_op jit(solution)/shard_map/all_gather | solution.py:61
  319.1 19.2 %add_convert_fusion = bf16[4096,2,1024]{2,1,0:T(2,128)(2,1)S(1)} fusion(bf16[4096,2,1024]{2,1,0:T(2,128)(2,1)} %all-gather.3.cloned.1.call-done, bf16[4096,2,1024]{2,1,0:T(2,128)(2,1)} %param.21), kind=kLoop, calls=%fused_computation | loop fusion | flops 33554432 | bytes 50331648 | tf_op jit(solution)/shard_map/convert_element_type | solution.py:64
  338.3 9.3 %copy.40 = bf16[512,8,2,1024]{3,1,2,0:T(8,128)(2,1)} copy(bf16[512,8,2,1024]{3,2,1,0:T(2,128)(2,1)S(1)} %bitcast.210) | data formatting | bytes 33554432
  347.6 20.7 %copy.31 = bf16[2048,4096]{1,0:T(8,128)(2,1)} copy(bf16[2048,4096]{0,1:T(8,128)(2,1)} %bitcast.211) | data formatting | bytes 33554432 | tf_op jit(solution)/shard_map/dot_general | solution.py:87
  368.3 10.2 %fusion.29 = f32[8,2,1024]{2,0,1:T(8,128)S(1)} fusion(bf16[2,1024,4096]{2,1,0:T(8,128)(2,1)} %bitcast.206, f32[4096]{0:T(1024)S(1)} %copy-done.5, f32[8]{0:T(128)S(1)} %add_rsqrt_fusion.7, bf16[4,8,4096]{2,1,0:T(8,128)(2,1)S(1)} %copy-done.2), kind=kOutput, calls=%fused_computation.67 | convolution fusion | flops 134348800 | bytes 16925184 | tf_op jit(solution)/shard_map/dot_general | solution.py:87
  378.8 13.1 %fusion.1 = f32[8,1,16,64]{3,1,2,0:T(1,128)S(1)} fusion(f32[8,16,64,256]{3,2,1,0:T(8,128)} %param.33, f32[8,256]{1,0:T(8,128)S(1)} %get-tuple-element.23, f32[8,16,64]{2,1,0:T(8,128)S(1)} %broadcast_multiply_fusion.3, f32[8,16]{1,0:T(8,128)S(1)} %get-tuple-element.26, f32[8,256,1,1]{1,0,2,3:T(8,128)S(1)} %get-tuple-element.22), kind=kOutput, calls=%fused_computation.9 | convolution fusion | flops 31457280 | bytes 8471040 | tf_op jit(solution)/shard_map/rhpn,rn->rhp/dot_general | solution.py:106
  391.9 0.2 multiply_reduce_fusion.6
  392.2 16.4 %psum.56 = f32[8,4]{0,1:T(4,128)S(1)} all-reduce(f32[8,4]{0,1:T(4,128)S(1)} %broadcast_multiply_fusion.7), channel_id=1, replica_groups=mesh['dp'=4,'tp'=8] {'tp'}, use_global_device_ids=true, to_apply=%region_4.5 | all-reduce | flops 32 | bytes 256 | tf_op jit(solution)/shard_map/psum | solution.py:111
  408.8 4.6 fusion.84
  413.4 27.1 %all-reduce.4 = bf16[8,4096]{1,0:T(8,128)(2,1)S(1)} all-reduce(f32[8,4096]{1,0:T(8,128)S(1)} %fusion.84), channel_id=1, replica_groups=mesh['dp'=4,'tp'=8] {'tp'}, use_global_device_ids=true, to_apply=%region_6.7 | all-reduce | flops 32768 | bytes 196608 | tf_op jit(solution)/shard_map/psum | solution.py:115
  440.5 0.1 multiply_reduce_fusion.2
  440.7 0.1 multiply_convert_fusion.2
  440.8 10.2 %fusion.35 = f32[8,2,1024]{2,0,1:T(8,128)S(1)} fusion(bf16[2,1024,4096]{2,1,0:T(8,128)(2,1)} %bitcast.207, bf16[8,4096]{1,0:T(8,128)(2,1)S(1)} %multiply_convert_fusion.2), kind=kOutput, calls=%fused_computation.72 | convolution fusion | flops 134217728 | bytes 16908288 | tf_op jit(solution)/shard_map/dot_general | solution.py:87
  451.0 0.2 multiply_exponential_fusion.3
  451.2 0.4 convolution_bitcast_fusion.2
  451.7 14.0 %all_gather.21 = f32[8,2048]{1,0:T(8,128)S(1)} all-gather(f32[8,256]{1,0:T(8,128)S(1)} %divide_multiply_fusion.6), channel_id=1, replica_groups=mesh['dp'=4,'tp'=8] {'tp'}, dimensions={1}, use_global_device_ids=true | all-gather | bytes 73728 | tf_op jit(solution)/shard_map/all_gather | solution.py:95
  465.9 13.7 %fusion.10 = f32[8,1,16,64]{3,1,2,0:T(1,128)S(1)} fusion(f32[8,16,64,256]{3,2,1,0:T(8,128)} %param.33, f32[8,256]{1,0:T(8,128)S(1)} %get-tuple-element.19, f32[8,16,64]{2,1,0:T(8,128)S(1)} %broadcast_multiply_fusion.2, f32[8,16]{1,0:T(8,128)S(1)} %get-tuple-element.28, f32[8,256]{1,0:T(8,128)S(1)} %get-tuple-element.23, ...), kind=kOutput, calls=%fused_computation.19 | convolution fusion | flops 37748736 | bytes 8512512 | tf_op jit(solution)/shard_map/rhpn,rn->rhp/dot_general | solution.py:106
  479.5 0.2 multiply_reduce_fusion.5
  479.9 13.9 %psum.58 = f32[8,4]{0,1:T(4,128)S(1)} all-reduce(f32[8,4]{0,1:T(4,128)S(1)} %broadcast_multiply_fusion.6), channel_id=1, replica_groups=mesh['dp'=4,'tp'=8] {'tp'}, use_global_device_ids=true, to_apply=%region_11.12 | all-reduce | flops 32 | bytes 256 | tf_op jit(solution)/shard_map/psum | solution.py:111
  493.8 0.1 multiply_reduce_fusion.9
  493.9 4.6 fusion.82
  498.6 27.7 %all-reduce.5 = bf16[8,4096]{1,0:T(8,128)(2,1)S(1)} all-reduce(f32[8,4096]{1,0:T(8,128)S(1)} %fusion.82), channel_id=1, replica_groups=mesh['dp'=4,'tp'=8] {'tp'}, use_global_device_ids=true, to_apply=%region_13.14 | all-reduce | flops 32768 | bytes 196608 | tf_op jit(solution)/shard_map/psum | solution.py:115
  526.2 0.1 multiply_reduce_fusion.1
  526.4 0.1 multiply_convert_fusion.1
  526.5 10.2 %fusion.33 = f32[8,2,1024]{2,0,1:T(8,128)S(1)} fusion(bf16[2,1024,4096]{2,1,0:T(8,128)(2,1)} %bitcast.208, bf16[8,4096]{1,0:T(8,128)(2,1)S(1)} %multiply_convert_fusion.1), kind=kOutput, calls=%fused_computation.70 | convolution fusion | flops 134217728 | bytes 16908288 | tf_op jit(solution)/shard_map/dot_general | solution.py:87
  536.7 0.2 multiply_exponential_fusion.2
  536.9 0.4 convolution_bitcast_fusion.1
  537.4 14.0 %all_gather.22 = f32[8,2048]{1,0:T(8,128)S(1)} all-gather(f32[8,256]{1,0:T(8,128)S(1)} %divide_multiply_fusion.5), channel_id=1, replica_groups=mesh['dp'=4,'tp'=8] {'tp'}, dimensions={1}, use_global_device_ids=true | all-gather | bytes 73728 | tf_op jit(solution)/shard_map/all_gather | solution.py:95
  551.6 14.5 %fusion.2 = f32[8,1,16,64]{3,1,2,0:T(1,128)S(1)} fusion(f32[8,256]{1,0:T(8,128)S(1)} %get-tuple-element.15, f32[8,16,64]{2,1,0:T(8,128)S(1)} %broadcast_multiply_fusion.1, f32[8,16]{1,0:T(8,128)S(1)} %get-tuple-element.30, f32[8,16,64,256]{3,2,1,0:T(8,128)} %param.33, f32[8,256]{1,0:T(8,128)S(1)} %get-tuple-element.19, ...), kind=kOutput, calls=%fused_computation.10 | convolution fusion | flops 44040192 | bytes 8553984 | tf_op jit(solution)/shard_map/rhpn,rn->rhp/dot_general | solution.py:106
  566.1 0.2 multiply_reduce_fusion.4
  566.4 13.9 %psum.60 = f32[8,4]{0,1:T(4,128)S(1)} all-reduce(f32[8,4]{0,1:T(4,128)S(1)} %broadcast_multiply_fusion.5), channel_id=1, replica_groups=mesh['dp'=4,'tp'=8] {'tp'}, use_global_device_ids=true, to_apply=%region_18.19 | all-reduce | flops 32 | bytes 256 | tf_op jit(solution)/shard_map/psum | solution.py:111
  580.3 0.1 multiply_reduce_fusion.8
  580.5 4.6 fusion.80
  585.1 27.2 %all-reduce.6 = bf16[8,4096]{1,0:T(8,128)(2,1)S(1)} all-reduce(f32[8,4096]{1,0:T(8,128)S(1)} %fusion.80), channel_id=1, replica_groups=mesh['dp'=4,'tp'=8] {'tp'}, use_global_device_ids=true, to_apply=%region_20.21 | all-reduce | flops 32768 | bytes 196608 | tf_op jit(solution)/shard_map/psum | solution.py:115
  612.3 0.1 multiply_reduce_fusion
  612.5 0.1 multiply_convert_fusion
  612.6 10.2 %fusion.31 = f32[8,2,1024]{2,0,1:T(8,128)S(1)} fusion(bf16[2,1024,4096]{2,1,0:T(8,128)(2,1)} %bitcast.209, bf16[8,4096]{1,0:T(8,128)(2,1)S(1)} %multiply_convert_fusion), kind=kOutput, calls=%fused_computation.68 | convolution fusion | flops 134217728 | bytes 16908288 | tf_op jit(solution)/shard_map/dot_general | solution.py:87
  622.8 0.2 multiply_exponential_fusion.1
  623.0 0.4 convolution_bitcast_fusion
  623.5 14.2 %all_gather.23 = f32[8,2048]{1,0:T(8,128)S(1)} all-gather(f32[8,256]{1,0:T(8,128)S(1)} %divide_multiply_fusion.4), channel_id=1, replica_groups=mesh['dp'=4,'tp'=8] {'tp'}, dimensions={1}, use_global_device_ids=true | all-gather | bytes 73728 | tf_op jit(solution)/shard_map/all_gather | solution.py:95
  637.8 7.7 %multiply_add_fusion = f32[8,16,64,256]{3,2,1,0:T(8,128)S(1)} fusion(f32[8,256]{1,0:T(8,128)S(1)} %get-tuple-element.11, f32[8,16,64]{2,1,0:T(8,128)S(1)} %broadcast_multiply_fusion, f32[8,16]{1,0:T(8,128)S(1)} %get-tuple-element.32, f32[8,256]{1,0:T(8,128)S(1)} %get-tuple-element.15, f32[8,16,64]{2,1,0:T(8,128)S(1)} %broadcast_multiply_fusion.1, ...), kind=kLoop, calls=%fused_computation.5 | loop fusion | flops 25165824 | bytes 16943104 | tf_op jit(solution)/shard_map/add | solution.py:102
  645.5 3.4 copy-done.1
  648.9 9.8 %fusion.99 = f32[8,1,16,64]{3,1,2,0:T(1,128)S(1)} fusion(f32[8,16,64,256]{3,2,1,0:T(8,128)S(1)} %multiply_add_fusion, f32[8,256,1,1]{1,0,2,3:T(8,128)S(1)} %get-tuple-element.10), kind=kOutput, calls=%fused_computation.172 | convolution fusion | flops 25165824 | bytes 8429568 | tf_op jit(solution)/shard_map/rhpn,rn->rhp/dot_general | solution.py:106
  658.8 0.2 multiply_reduce_fusion.3
  659.1 13.9 %psum.62 = f32[8,4]{0,1:T(4,128)S(1)} all-reduce(f32[8,4]{0,1:T(4,128)S(1)} %broadcast_multiply_fusion.4), channel_id=1, replica_groups=mesh['dp'=4,'tp'=8] {'tp'}, use_global_device_ids=true, to_apply=%region_25.26 | all-reduce | flops 32 | bytes 256 | tf_op jit(solution)/shard_map/psum | solution.py:111
  673.2 4.6 fusion.78
  677.8 27.2 %all-reduce.7 = bf16[8,4096]{1,0:T(8,128)(2,1)S(1)} all-reduce(f32[8,4096]{1,0:T(8,128)S(1)} %fusion.78), channel_id=1, replica_groups=mesh['dp'=4,'tp'=8] {'tp'}, use_global_device_ids=true, to_apply=%region_27.28 | all-reduce | flops 32768 | bytes 196608 | tf_op jit(solution)/shard_map/psum | solution.py:115
  705.0 0.6 pad_maximum_fusion.6
  (101 shorter events, 2.5 us)
Async XLA Ops:
  7.2 156.0 %copy-start = (bf16[4096,256]{1,0:T(8,128)(2,1)S(1)}, bf16[4096,256]{1,0:T(8,128)(2,1)}, u32[]{:S(2)}) copy-start(bf16[4096,256]{1,0:T(8,128)(2,1)} %param.24) | copy-start | bytes 6291460
  7.2 170.9 %all-gather.5.cloned.1.call-start = ((), (), s32[]{:S(2)}) async-start(), calls=%async_computation.2 | async-start | bytes 10485760 | tf_op jit(solution)/shard_map/all_gather | solution.py:68
  12.6 21.5 %copy-start.10 = (s32[8,2,8]{2,1,0:T(2,128)S(1)}, s32[8,2,8]{2,1,0:T(2,128)}, u32[]{:S(2)}) copy-start(s32[8,2,8]{2,1,0:T(2,128)} %param.23) | copy-start | bytes 1540
  27.6 100.5 %all-to-all-start = ((bf16[128,2,8192]{0,1,2:T(2,128)(2,1)}), bf16[128,2,8192]{0,1,2:T(2,128)(2,1)}, u32[]{:S(2)}, u32[]{:S(2)}) async-start(bf16[128,2,8192]{0,1,2:T(2,128)(2,1)} %copy.29), calls=%async_computation | async-start | bytes 8388608 | tf_op jit(solution)/shard_map/all_to_all | solution.py:58
  34.0 285.2 %all-gather.3.cloned.1.call-start = ((), (), s32[]{:S(2)}) async-start(), calls=%async_computation.1 | async-start | bytes 20971520 | tf_op jit(solution)/shard_map/all_gather | solution.py:61
  153.6 9.1 %copy-start.13 = (f32[5,256]{1,0:T(8,128)S(1)}, f32[5,256]{1,0:T(8,128)}, u32[]{:S(2)}) copy-start(f32[5,256]{1,0:T(8,128)} %param.27) | copy-start | bytes 15364
  153.6 9.2 %copy-start.8 = (bf16[8,3,256]{2,0,1:T(8,128)(2,1)S(1)}, bf16[8,3,256]{2,0,1:T(8,128)(2,1)}, u32[]{:S(2)}) copy-start(bf16[8,3,256]{2,0,1:T(8,128)(2,1)} %param.32) | copy-start | bytes 36868
  153.6 9.2 %copy-start.7 = (f32[5,1024]{1,0:T(8,128)S(1)}, f32[5,1024]{1,0:T(8,128)}, u32[]{:S(2)}) copy-start(f32[5,1024]{1,0:T(8,128)} %param.26) | copy-start | bytes 61444
  153.6 9.2 %copy-start.6 = (bf16[8,3,1024]{2,0,1:T(8,128)(2,1)S(1)}, bf16[8,3,1024]{2,0,1:T(8,128)(2,1)}, u32[]{:S(2)}) copy-start(bf16[8,3,1024]{2,0,1:T(8,128)(2,1)} %param.31) | copy-start | bytes 147460
  153.6 9.3 %copy-start.2 = (bf16[4,8,4096]{2,1,0:T(8,128)(2,1)S(1)}, bf16[4,8,4096]{2,1,0:T(8,128)(2,1)}, u32[]{:S(2)}) copy-start(bf16[4,8,4096]{2,1,0:T(8,128)(2,1)} %param.19) | copy-start | bytes 786436
  153.6 9.5 %copy-start.5 = (f32[4096]{0:T(1024)S(1)}, f32[4096]{0:T(1024)}, u32[]{:S(2)}) copy-start(f32[4096]{0:T(1024)} %param.20) | copy-start | bytes 49156
  153.7 24.1 %copy-start.3 = (bf16[4096,16]{0,1:T(8,128)(2,1)S(1)}, bf16[4096,16]{0,1:T(8,128)(2,1)}, u32[]{:S(2)}) copy-start(bf16[4096,16]{0,1:T(8,128)(2,1)} %param.25) | copy-start | bytes 393220
  153.7 24.1 %copy-start.11 = (f32[16]{0:T(128)S(1)}, f32[16]{0:T(128)}, u32[]{:S(2)}) copy-start(f32[16]{0:T(128)} %param.29) | copy-start | bytes 196
  153.7 24.1 %copy-start.12 = (f32[16]{0:T(128)S(1)}, f32[16]{0:T(128)}, u32[]{:S(2)}) copy-start(f32[16]{0:T(128)} %param.28) | copy-start | bytes 196
  378.5 13.4 %copy-start.9 = (f32[16]{0:T(128)S(1)}, f32[16]{0:T(128)}, u32[]{:S(2)}) copy-start(f32[16]{0:T(128)} %param.30) | copy-start | bytes 196
  378.5 30.2 %copy-start.4 = (f32[1024]{0:T(1024)S(1)}, f32[1024]{0:T(1024)}, u32[]{:S(2)}) copy-start(f32[1024]{0:T(1024)} %param.34) | copy-start | bytes 12292
  645.5 3.4 copy-start.1
Sparse Core Ops, SparseCore 0:
  12.7 90.1 all-gather.4
  162.9 156.2 all-gather.2
where the time goes:
time: 721 us; the launch traced here: 713 us
  blocking collectives  224 us (31%)
  waiting for transfers between devices  210 us (29%)
  matrix products  113 us (16%)
  local copies, waits for them, and re-layouts  81.8 us (11%)
  other arithmetic  63.1 us (9%)
  between operations  14.8 us (2%)
    all_gather x1, waiting for transfers between devices, body(): lax.all_gather(zx_delta.astype(jnp.bfloat16), 'dp', axis=0, tiled=True)  131 us
    psum x4, blocking collectives, body(): whole = lax.psum(partial_value, 'tp').astype(jnp.bfloat16)  109 us
    all_to_all x1, waiting for transfers between devices, body(): lax.all_to_all(zx_codes, 'tp', split_axis=2, concat_axis=0, tiled=True)  79.2 us
    psum x4, blocking collectives, body(): totals = lax.psum(squares[:, None] * group_mask, 'tp')  58.1 us
    all_gather x4, blocking collectives, body(): bc_all = lax.all_gather(conv_piece, 'tp', axis=1, tiled=True)  56.3 us
    dot_general x4, matrix products, body(): jnp.einsum('rhpn,rn->rhp', state, c_group, precision=lax.Precision.HIGHEST)  51.1 us
    dot_general x4, matrix products, body(): zx = jnp.dot(normed, zx_weights, preferred_element_type=jnp.float32)  40.7 us
    unnamed x30, local copies, waits for them, and re-layouts  27.7 us
  transfers between devices with their start and end apart: 3, of which 2 were waited for; matrix products, arithmetic and copies ran while one was open for 11% of the time, Pallas kernels for 0%

commit v1 on v0

--- a/solution.py
+++ b/solution.py
@@ -55,7 +55,9 @@
 ):
     slot = lax.axis_index("tp")
     tp_count = lax.axis_size("tp")
-    traded = lax.all_to_all(zx_codes, "tp", split_axis=2, concat_axis=0, tiled=True)
+    traded = jnp.concatenate(
+        lax.all_to_all(jnp.stack(jnp.split(zx_codes, lax.axis_size("tp"), 2)), "tp", 0, 0), 0
+    )
     zx_delta = decode_pairs(traded, zx_exponents, BLK)
     local_cols = traded.shape[2]
     gathered = lax.all_gather(zx_delta.astype(jnp.bfloat16), "dp", axis=0, tiled=True)

time: 721 us -> 696 us (0.965)
  local copies, waits for them, and re-layouts: 81.8 us -> 67.6 us
  other arithmetic: 63.1 us -> 53.8 us
    convert_element_type x1 -> x0, local copies, waits for them, and re-layouts: 17.1 us -> none  [decode_pairs(): codes.astype(jnp.float32)]
    convert_element_type x1 -> x0, other arithmetic: 8.47 us -> none  [decode_pairs(): codes.astype(jnp.float32)]
    unnamed x30 -> x36, local copies, waits for them, and re-layouts: 27.7 us -> 28.5 us
  transfers between devices with their start and end apart: 3 -> 3, of which waited for: 2 -> 2; matrix products, arithmetic and copies ran while one was open for 11% -> 8% of each run, Pallas kernels for 0% -> 0%
where the time goes in v1:
time: 696 us; the launch traced here: 689 us
  blocking collectives  224 us (32%)
  waiting for transfers between devices  210 us (30%)
  matrix products  113 us (16%)
  local copies, waits for them, and re-layouts  67.6 us (10%)
  other arithmetic  53.8 us (8%)
  between operations  14.8 us (2%)
    all_gather x1, waiting for transfers between devices, body(): lax.all_gather(zx_delta.astype(jnp.bfloat16), 'dp', axis=0, tiled=True)  131 us
    psum x4, blocking collectives, body(): whole = lax.psum(partial_value, 'tp').astype(jnp.bfloat16)  109 us
    all_to_all x1, waiting for transfers between devices, body(): lax.all_to_all(jnp.stack(jnp.split(zx_codes, lax.axis_size('tp'), 2)), 't...  79.2 us
    psum x4, blocking collectives, body(): totals = lax.psum(squares[:, None] * group_mask, 'tp')  58.1 us
    all_gather x4, blocking collectives, body(): bc_all = lax.all_gather(conv_piece, 'tp', axis=1, tiled=True)  56.3 us
    dot_general x4, matrix products, body(): jnp.einsum('rhpn,rn->rhp', state, c_group, precision=lax.Precision.HIGHEST)  51.1 us
    dot_general x4, matrix products, body(): zx = jnp.dot(normed, zx_weights, preferred_element_type=jnp.float32)  40.7 us
    unnamed x36, local copies, waits for them, and re-layouts  28.5 us
  transfers between devices with their start and end apart: 3, of which 2 were waited for; matrix products, arithmetic and copies ran while one was open for 8% of the time, Pallas kernels for 0%

profile of v1, /device:TPU:0, one launch (start us, length us, event | category | flops | bytes accessed | tf_op | source)
XLA Modules:
  0.0 688.9 jit_solution(703670501271488166)
XLA Ops:
  7.2 0.8 multiply_exponential_fusion.4
  8.1 0.3 mul.639
  8.4 4.1 fusion.3
  12.6 2.2 bitcast_dynamic-update-slice_fusion.7
  14.8 2.2 bitcast_dynamic-update-slice_fusion.6
  17.1 2.2 bitcast_dynamic-update-slice_fusion.5
  19.2 2.2 bitcast_dynamic-update-slice_fusion.4
  21.4 2.3 bitcast_dynamic-update-slice_fusion.3
  23.8 2.3 bitcast_dynamic-update-slice_fusion.2
  26.0 2.3 bitcast_dynamic-update-slice_fusion.1
  28.4 2.2 bitcast_dynamic-update-slice_fusion
  30.6 6.2 all-to-all-start
  36.8 4.0 mul.609
  40.8 10.8 %mul.610 = f32[1024,2,1024]{2,1,0:T(2,128)} reshape(f32[8,128,2,8,128]{4,3,2,1,0:T(8,128)} %mul.609) | data formatting | bytes 16777216 | tf_op jit(solution)/shard_map/mul | solution.py:19
  51.7 79.2 %all-to-all-done = bf16[8,128,2,1024]{3,2,1,0:T(2,128)(2,1)} async-done(((bf16[8,128,2,1024]{3,2,1,0:T(2,128)(2,1)}), bf16[8,128,2,1024]{3,2,1,0:T(2,128)(2,1)}, u32[]{:S(2)}, u32[]{:S(2)}) %all-to-all-start) | async-done | bytes 4194336 | tf_op jit(solution)/shard_map/all_to_all | solution.py:59
  130.8 8.1 %fusion = bf16[1024,2,1024]{2,1,0:T(2,128)(2,1)} fusion(f32[1024,2,1024]{2,1,0:T(2,128)} %mul.610, bf16[8,128,2,1024]{3,2,1,0:T(2,128)(2,1)} %all-to-all-done), kind=kLoop, calls=%fused_computation.3 | loop fusion | flops 6291456 | bytes 16777216 | tf_op jit(solution)/shard_map/convert_element_type | solution.py:63
  139.2 0.1 fusion.13
  139.4 0.4 convolution_bitcast_fusion.3
  139.8 14.2 %all_gather.19 = f32[8,2048]{1,0:T(8,128)S(1)} all-gather(f32[8,256]{1,0:T(8,128)S(1)} %divide_multiply_fusion.7), channel_id=1, replica_groups=mesh['dp'=4,'tp'=8] {'tp'}, dimensions={1}, use_global_device_ids=true | all-gather | bytes 73728 | tf_op jit(solution)/shard_map/all_gather | solution.py:97
  154.0 0.2 multiply_exponential_fusion.5
  154.3 10.1 %add_convert_fusion.1 = bf16[1024,4096]{1,0:T(8,128)(2,1)} fusion(bf16[1024,4096]{1,0:T(8,128)(2,1)} %all-gather.5.cloned.1.call-done, bf16[1024,4096]{1,0:T(8,128)(2,1)} %param.35), kind=kLoop, calls=%fused_computation.1 | loop fusion | flops 16777216 | bytes 25165824 | tf_op jit(solution)/shard_map/convert_element_type | solution.py:71
  164.4 131.0 %all-gather.3.cloned.1.call-done = bf16[4096,2,1024]{2,1,0:T(2,128)(2,1)} async-done(((bf16[1024,2,1024]{2,1,0:T(2,128)(2,1)}), bf16[4096,2,1024]{2,1,0:T(2,128)(2,1)}) %all-gather.3.cloned.1.call-update) | async-done | bytes 16777232 | tf_op jit(solution)/shard_map/all_gather | solution.py:63
  295.4 19.2 %add_convert_fusion = bf16[4096,2,1024]{2,1,0:T(2,128)(2,1)S(1)} fusion(bf16[4096,2,1024]{2,1,0:T(2,128)(2,1)} %all-gather.3.cloned.1.call-done, bf16[4096,2,1024]{2,1,0:T(2,128)(2,1)} %param.21), kind=kLoop, calls=%fused_computation | loop fusion | flops 33554432 | bytes 50331648 | tf_op jit(solution)/shard_map/convert_element_type | solution.py:66
  314.6 9.3 %copy.32 = bf16[512,8,2,1024]{3,1,2,0:T(8,128)(2,1)} copy(bf16[512,8,2,1024]{3,2,1,0:T(2,128)(2,1)S(1)} %bitcast.221) | data formatting | bytes 33554432
  323.9 20.7 %copy.23 = bf16[2048,4096]{1,0:T(8,128)(2,1)} copy(bf16[2048,4096]{0,1:T(8,128)(2,1)} %bitcast.222) | data formatting | bytes 33554432 | tf_op jit(solution)/shard_map/dot_general | solution.py:89
  344.6 10.2 %fusion.29 = f32[8,2,1024]{2,0,1:T(8,128)S(1)} fusion(bf16[2,1024,4096]{2,1,0:T(8,128)(2,1)} %bitcast.217, f32[4096]{0:T(1024)S(1)} %copy-done.5, f32[8]{0:T(128)S(1)} %add_rsqrt_fusion.7, bf16[4,8,4096]{2,1,0:T(8,128)(2,1)S(1)} %copy-done.2), kind=kOutput, calls=%fused_computation.74 | convolution fusion | flops 134348800 | bytes 16925184 | tf_op jit(solution)/shard_map/dot_general | solution.py:89
  355.1 13.1 %fusion.1 = f32[8,1,16,64]{3,1,2,0:T(1,128)S(1)} fusion(f32[8,16,64,256]{3,2,1,0:T(8,128)} %param.33, f32[8,256]{1,0:T(8,128)S(1)} %get-tuple-element.23, f32[8,16,64]{2,1,0:T(8,128)S(1)} %broadcast_multiply_fusion.3, f32[8,16]{1,0:T(8,128)S(1)} %get-tuple-element.26, f32[8,256,1,1]{1,0,2,3:T(8,128)S(1)} %get-tuple-element.22), kind=kOutput, calls=%fused_computation.8 | convolution fusion | flops 31457280 | bytes 8471040 | tf_op jit(solution)/shard_map/rhpn,rn->rhp/dot_general | solution.py:108
  368.1 0.2 multiply_reduce_fusion.6
  368.4 16.4 %psum.56 = f32[8,4]{0,1:T(4,128)S(1)} all-reduce(f32[8,4]{0,1:T(4,128)S(1)} %broadcast_multiply_fusion.7), channel_id=1, replica_groups=mesh['dp'=4,'tp'=8] {'tp'}, use_global_device_ids=true, to_apply=%region_4.5 | all-reduce | flops 32 | bytes 256 | tf_op jit(solution)/shard_map/psum | solution.py:113
  385.0 4.6 fusion.84
  389.6 27.1 %all-reduce.4 = bf16[8,4096]{1,0:T(8,128)(2,1)S(1)} all-reduce(f32[8,4096]{1,0:T(8,128)S(1)} %fusion.84), channel_id=1, replica_groups=mesh['dp'=4,'tp'=8] {'tp'}, use_global_device_ids=true, to_apply=%region_6.7 | all-reduce | flops 32768 | bytes 196608 | tf_op jit(solution)/shard_map/psum | solution.py:117
  416.8 0.1 multiply_reduce_fusion.2
  417.0 10.2 %fusion.35 = f32[8,2,1024]{2,0,1:T(8,128)S(1)} fusion(bf16[2,1024,4096]{2,1,0:T(8,128)(2,1)} %bitcast.218, bf16[8,4096]{1,0:T(8,128)(2,1)S(1)} %multiply_convert_fusion.2), kind=kOutput, calls=%fused_computation.79 | convolution fusion | flops 134217728 | bytes 16908288 | tf_op jit(solution)/shard_map/dot_general | solution.py:89
  427.3 0.2 multiply_exponential_fusion.3
  427.4 0.4 convolution_bitcast_fusion.2
  427.9 14.0 %all_gather.21 = f32[8,2048]{1,0:T(8,128)S(1)} all-gather(f32[8,256]{1,0:T(8,128)S(1)} %divide_multiply_fusion.6), channel_id=1, replica_groups=mesh['dp'=4,'tp'=8] {'tp'}, dimensions={1}, use_global_device_ids=true | all-gather | bytes 73728 | tf_op jit(solution)/shard_map/all_gather | solution.py:97
  442.1 13.7 %fusion.10 = f32[8,1,16,64]{3,1,2,0:T(1,128)S(1)} fusion(f32[8,16,64,256]{3,2,1,0:T(8,128)} %param.33, f32[8,256]{1,0:T(8,128)S(1)} %get-tuple-element.19, f32[8,16,64]{2,1,0:T(8,128)S(1)} %broadcast_multiply_fusion.2, f32[8,16]{1,0:T(8,128)S(1)} %get-tuple-element.28, f32[8,256]{1,0:T(8,128)S(1)} %get-tuple-element.23, ...), kind=kOutput, calls=%fused_computation.18 | convolution fusion | flops 37748736 | bytes 8512512 | tf_op jit(solution)/shard_map/rhpn,rn->rhp/dot_general | solution.py:108
  455.8 0.2 multiply_reduce_fusion.5
  456.1 13.9 %psum.58 = f32[8,4]{0,1:T(4,128)S(1)} all-reduce(f32[8,4]{0,1:T(4,128)S(1)} %broadcast_multiply_fusion.6), channel_id=1, replica_groups=mesh['dp'=4,'tp'=8] {'tp'}, use_global_device_ids=true, to_apply=%region_11.12 | all-reduce | flops 32 | bytes 256 | tf_op jit(solution)/shard_map/psum | solution.py:113
  470.2 4.6 fusion.82
  474.8 27.7 %all-reduce.5 = bf16[8,4096]{1,0:T(8,128)(2,1)S(1)} all-reduce(f32[8,4096]{1,0:T(8,128)S(1)} %fusion.82), channel_id=1, replica_groups=mesh['dp'=4,'tp'=8] {'tp'}, use_global_device_ids=true, to_apply=%region_13.14 | all-reduce | flops 32768 | bytes 196608 | tf_op jit(solution)/shard_map/psum | solution.py:117
  502.5 0.1 multiply_reduce_fusion.1
  502.7 10.2 %fusion.33 = f32[8,2,1024]{2,0,1:T(8,128)S(1)} fusion(bf16[2,1024,4096]{2,1,0:T(8,128)(2,1)} %bitcast.219, bf16[8,4096]{1,0:T(8,128)(2,1)S(1)} %multiply_convert_fusion.1), kind=kOutput, calls=%fused_computation.77 | convolution fusion | flops 134217728 | bytes 16908288 | tf_op jit(solution)/shard_map/dot_general | solution.py:89
  513.0 0.2 multiply_exponential_fusion.2
  513.1 0.4 convolution_bitcast_fusion.1
  513.6 14.0 %all_gather.22 = f32[8,2048]{1,0:T(8,128)S(1)} all-gather(f32[8,256]{1,0:T(8,128)S(1)} %divide_multiply_fusion.5), channel_id=1, replica_groups=mesh['dp'=4,'tp'=8] {'tp'}, dimensions={1}, use_global_device_ids=true | all-gather | bytes 73728 | tf_op jit(solution)/shard_map/all_gather | solution.py:97
  527.8 14.5 %fusion.2 = f32[8,1,16,64]{3,1,2,0:T(1,128)S(1)} fusion(f32[8,256]{1,0:T(8,128)S(1)} %get-tuple-element.15, f32[8,16,64]{2,1,0:T(8,128)S(1)} %broadcast_multiply_fusion.1, f32[8,16]{1,0:T(8,128)S(1)} %get-tuple-element.30, f32[8,16,64,256]{3,2,1,0:T(8,128)} %param.33, f32[8,256]{1,0:T(8,128)S(1)} %get-tuple-element.19, ...), kind=kOutput, calls=%fused_computation.9 | convolution fusion | flops 44040192 | bytes 8553984 | tf_op jit(solution)/shard_map/rhpn,rn->rhp/dot_general | solution.py:108
  542.3 0.2 multiply_reduce_fusion.4
  542.6 13.9 %psum.60 = f32[8,4]{0,1:T(4,128)S(1)} all-reduce(f32[8,4]{0,1:T(4,128)S(1)} %broadcast_multiply_fusion.5), channel_id=1, replica_groups=mesh['dp'=4,'tp'=8] {'tp'}, use_global_device_ids=true, to_apply=%region_18.19 | all-reduce | flops 32 | bytes 256 | tf_op jit(solution)/shard_map/psum | solution.py:113
  556.7 4.6 fusion.80
  561.3 27.2 %all-reduce.6 = bf16[8,4096]{1,0:T(8,128)(2,1)S(1)} all-reduce(f32[8,4096]{1,0:T(8,128)S(1)} %fusion.80), channel_id=1, replica_groups=mesh['dp'=4,'tp'=8] {'tp'}, use_global_device_ids=true, to_apply=%region_20.21 | all-reduce | flops 32768 | bytes 196608 | tf_op jit(solution)/shard_map/psum | solution.py:117
  588.6 0.1 multiply_reduce_fusion
  588.8 10.2 %fusion.31 = f32[8,2,1024]{2,0,1:T(8,128)S(1)} fusion(bf16[2,1024,4096]{2,1,0:T(8,128)(2,1)} %bitcast.220, bf16[8,4096]{1,0:T(8,128)(2,1)S(1)} %multiply_convert_fusion), kind=kOutput, calls=%fused_computation.75 | convolution fusion | flops 134217728 | bytes 16908288 | tf_op jit(solution)/shard_map/dot_general | solution.py:89
  599.0 0.2 multiply_exponential_fusion.1
  599.2 0.4 convolution_bitcast_fusion
  599.7 14.2 %all_gather.23 = f32[8,2048]{1,0:T(8,128)S(1)} all-gather(f32[8,256]{1,0:T(8,128)S(1)} %divide_multiply_fusion.4), channel_id=1, replica_groups=mesh['dp'=4,'tp'=8] {'tp'}, dimensions={1}, use_global_device_ids=true | all-gather | bytes 73728 | tf_op jit(solution)/shard_map/all_gather | solution.py:97
  614.1 7.7 %multiply_add_fusion = f32[8,16,64,256]{3,2,1,0:T(8,128)S(1)} fusion(f32[8,256]{1,0:T(8,128)S(1)} %get-tuple-element.11, f32[8,16,64]{2,1,0:T(8,128)S(1)} %broadcast_multiply_fusion, f32[8,16]{1,0:T(8,128)S(1)} %get-tuple-element.32, f32[8,256]{1,0:T(8,128)S(1)} %get-tuple-element.15, f32[8,16,64]{2,1,0:T(8,128)S(1)} %broadcast_multiply_fusion.1, ...), kind=kLoop, calls=%fused_computation.4 | loop fusion | flops 25165824 | bytes 16943104 | tf_op jit(solution)/shard_map/add | solution.py:104
  621.8 3.4 copy-done.1
  625.2 9.8 %fusion.99 = f32[8,1,16,64]{3,1,2,0:T(1,128)S(1)} fusion(f32[8,16,64,256]{3,2,1,0:T(8,128)S(1)} %multiply_add_fusion, f32[8,256,1,1]{1,0,2,3:T(8,128)S(1)} %get-tuple-element.10), kind=kOutput, calls=%fused_computation.179 | convolution fusion | flops 25165824 | bytes 8429568 | tf_op jit(solution)/shard_map/rhpn,rn->rhp/dot_general | solution.py:108
  635.0 0.2 multiply_reduce_fusion.3
  635.3 13.9 %psum.62 = f32[8,4]{0,1:T(4,128)S(1)} all-reduce(f32[8,4]{0,1:T(4,128)S(1)} %broadcast_multiply_fusion.4), channel_id=1, replica_groups=mesh['dp'=4,'tp'=8] {'tp'}, use_global_device_ids=true, to_apply=%region_25.26 | all-reduce | flops 32 | bytes 256 | tf_op jit(solution)/shard_map/psum | solution.py:113
  649.4 4.6 fusion.78
  654.0 27.2 %all-reduce.7 = bf16[8,4096]{1,0:T(8,128)(2,1)S(1)} all-reduce(f32[8,4096]{1,0:T(8,128)S(1)} %fusion.78), channel_id=1, replica_groups=mesh['dp'=4,'tp'=8] {'tp'}, use_global_device_ids=true, to_apply=%region_27.28 | all-reduce | flops 32768 | bytes 196608 | tf_op jit(solution)/shard_map/psum | solution.py:117
  681.3 0.6 pad_maximum_fusion.6
  (106 shorter events, 2.9 us)
Async XLA Ops:
  7.2 132.2 %copy-start = (bf16[4096,256]{1,0:T(8,128)(2,1)S(1)}, bf16[4096,256]{1,0:T(8,128)(2,1)}, u32[]{:S(2)}) copy-start(bf16[4096,256]{1,0:T(8,128)(2,1)} %param.24) | copy-start | bytes 6291460
  7.2 147.1 %all-gather.5.cloned.1.call-start = ((), (), s32[]{:S(2)}) async-start(), calls=%async_computation.2 | async-start | bytes 10485760 | tf_op jit(solution)/shard_map/all_gather | solution.py:70
  12.6 24.2 %copy-start.10 = (s32[8,2,8]{2,1,0:T(2,128)S(1)}, s32[8,2,8]{2,1,0:T(2,128)}, u32[]{:S(2)}) copy-start(s32[8,2,8]{2,1,0:T(2,128)} %param.23) | copy-start | bytes 1540
  30.6 100.3 %all-to-all-start = ((bf16[8,128,2,1024]{3,2,1,0:T(2,128)(2,1)}), bf16[8,128,2,1024]{3,2,1,0:T(2,128)(2,1)}, u32[]{:S(2)}, u32[]{:S(2)}) async-start(bf16[8,128,2,1024]{3,2,1,0:T(2,128)(2,1)} %bitcast_dynamic-update-slice_fusion), calls=%async_computation | async-start | bytes 8388608 | tf_op jit(solution)/shard_map/all_to_all | solution.py:59
  36.8 258.6 %all-gather.3.cloned.1.call-start = ((), (), s32[]{:S(2)}) async-start(), calls=%async_computation.1 | async-start | bytes 20971520 | tf_op jit(solution)/shard_map/all_gather | solution.py:63
  51.6 87.4 %copy-start.13 = (f32[5,256]{1,0:T(8,128)S(1)}, f32[5,256]{1,0:T(8,128)}, u32[]{:S(2)}) copy-start(f32[5,256]{1,0:T(8,128)} %param.27) | copy-start | bytes 15364
  51.6 87.4 %copy-start.8 = (bf16[8,3,256]{2,0,1:T(8,128)(2,1)S(1)}, bf16[8,3,256]{2,0,1:T(8,128)(2,1)}, u32[]{:S(2)}) copy-start(bf16[8,3,256]{2,0,1:T(8,128)(2,1)} %param.32) | copy-start | bytes 36868
  51.6 87.5 %copy-start.7 = (f32[5,1024]{1,0:T(8,128)S(1)}, f32[5,1024]{1,0:T(8,128)}, u32[]{:S(2)}) copy-start(f32[5,1024]{1,0:T(8,128)} %param.26) | copy-start | bytes 61444
  51.6 87.5 %copy-start.6 = (bf16[8,3,1024]{2,0,1:T(8,128)(2,1)S(1)}, bf16[8,3,1024]{2,0,1:T(8,128)(2,1)}, u32[]{:S(2)}) copy-start(bf16[8,3,1024]{2,0,1:T(8,128)(2,1)} %param.31) | copy-start | bytes 147460
  51.6 87.6 %copy-start.2 = (bf16[4,8,4096]{2,1,0:T(8,128)(2,1)S(1)}, bf16[4,8,4096]{2,1,0:T(8,128)(2,1)}, u32[]{:S(2)}) copy-start(bf16[4,8,4096]{2,1,0:T(8,128)(2,1)} %param.19) | copy-start | bytes 786436
  51.6 87.7 %copy-start.5 = (f32[4096]{0:T(1024)S(1)}, f32[4096]{0:T(1024)}, u32[]{:S(2)}) copy-start(f32[4096]{0:T(1024)} %param.20) | copy-start | bytes 49156
  51.6 102.4 %copy-start.3 = (bf16[4096,16]{0,1:T(8,128)(2,1)S(1)}, bf16[4096,16]{0,1:T(8,128)(2,1)}, u32[]{:S(2)}) copy-start(bf16[4096,16]{0,1:T(8,128)(2,1)} %param.25) | copy-start | bytes 393220
  51.7 102.4 %copy-start.11 = (f32[16]{0:T(128)S(1)}, f32[16]{0:T(128)}, u32[]{:S(2)}) copy-start(f32[16]{0:T(128)} %param.29) | copy-start | bytes 196
  51.7 102.4 %copy-start.12 = (f32[16]{0:T(128)S(1)}, f32[16]{0:T(128)}, u32[]{:S(2)}) copy-start(f32[16]{0:T(128)} %param.28) | copy-start | bytes 196
  354.7 13.4 %copy-start.9 = (f32[16]{0:T(128)S(1)}, f32[16]{0:T(128)}, u32[]{:S(2)}) copy-start(f32[16]{0:T(128)} %param.30) | copy-start | bytes 196
  354.7 30.2 %copy-start.4 = (f32[1024]{0:T(1024)S(1)}, f32[1024]{0:T(1024)}, u32[]{:S(2)}) copy-start(f32[1024]{0:T(1024)} %param.34) | copy-start | bytes 12292
  621.8 3.4 copy-start.1
Sparse Core Ops, SparseCore 0:
  12.7 90.1 all-gather.4
  139.1 156.2 all-gather.2
